TPU v7x, 32 devices: a whole 2x2x4 slice. The times are simulated.
32 devices in a mesh: dp: 8 (over y, x, core), tensor: 4 (over z).
Axes of the slice: x: 2, y: 2, z: 4, core: 2. Of those that a mesh axis runs over, the one named last changes fastest.
Arguments:
- hidden_in: bfloat16 [8, 1024, 2048], P('dp', 'tensor'), may hold values from -6 to 6
- cotangent: bfloat16 [8, 1024, 2048], P('dp', 'tensor'), may hold values from -6 to 6
- lengths: int32 [8], replicated, may hold values from 1 to 1024, 5632 in all
- slot_of_seq: int32 [8], replicated, may hold values from 0 to 7, as said below
- seq_of_slot: int32 [8], replicated, may hold values from 0 to 7, as said below
- qkv_weight: bfloat16 [2048, 3, 2048], P('dp', None, 'tensor'), may hold values from -0.125 to 0.125
- out_weight: bfloat16 [2048, 2048], P('dp', 'tensor'), may hold values from -0.75 to 0.75
- fc1_weight: bfloat16 [2048, 8192], P('dp', 'tensor'), may hold values from -0.125 to 0.125
- fc2_weight: bfloat16 [2048, 8192], P('dp', 'tensor'), may hold values from -0.0625 to 0.0625
- ln_gain: bfloat16 [2048], P(('dp', 'tensor')), may hold values from 0.5 to 1.5
- ln_bias: bfloat16 [2048], P(('dp', 'tensor')), may hold values from -3 to 3
- qkv_bias: bfloat16 [6144], P(('dp', 'tensor')), may hold values from -3 to 3
- out_bias: bfloat16 [2048], P(('dp', 'tensor')), may hold values from -3 to 3
- fc1_bias: bfloat16 [8192], P(('dp', 'tensor')), may hold values from -3 to 3
- fc2_bias: bfloat16 [2048], P(('dp', 'tensor')), may hold values from -3 to 3
Outputs:
- block_out: bfloat16 [8, 1024, 2048], P('dp', 'tensor')
- grad_input: bfloat16 [8, 1024, 2048], P('dp', 'tensor')
- grad_qkv_weight: float32 [2048, 3, 2048], P('dp', None, 'tensor')
- grad_out_weight: float32 [2048, 2048], P('dp', 'tensor')
- grad_fc1_weight: float32 [2048, 8192], P('dp', 'tensor')
- grad_fc2_weight: float32 [2048, 8192], P('dp', 'tensor')
- grad_ln_gain: float32 [2048], P(('dp', 'tensor'))
- grad_ln_bias: float32 [2048], P(('dp', 'tensor'))
- grad_qkv_bias: float32 [6144], P(('dp', 'tensor'))
- grad_out_bias: float32 [2048], P(('dp', 'tensor'))
- grad_fc1_bias: float32 [8192], P(('dp', 'tensor'))
- grad_fc2_bias: float32 [2048], P(('dp', 'tensor'))
Inputs may be any that keep to these rules, and one draw needn't show every extreme that they name: 8 lengths that sum to 5632, the longest exactly 1024; sequence s fills positions 0 to lengths[s] - 1. A permutation: sequence s is computed in slot slot_of_seq[s]; slot p lies on index p // 1 of dp. `seq_of_slot`: the inverse permutation of slot_of_seq.
All inputs are finite; a program needn't handle non-finite values.
Results may differ from a plain program's by a relative error of at most 0.0086.
Values may be sent and summed in bfloat16 or wider, within the bound.
No kernel may reach another device: no remote copies, remote signals or barrier semaphores. Data moves between devices by JAX's collectives and lax.ppermute only.
A program may use at most 256 MiB of HBM per device.

v0:
```python
import math
import jax
import jax.numpy as jnp
from jax import lax
from jax.sharding import PartitionSpec as P

HEAD_DIM = 64
ROT = 32
eps = 1e-05
masked_score = -1e30


def rotary_tables(row_count, col_count):
    half_rot = ROT // 2
    column = jnp.arange(col_count) % HEAD_DIM
    exponent = (2 * (column % half_rot)).astype(jnp.float32) / ROT
    frequency = jnp.exp(-math.log(10000.0) * exponent)
    angles = jnp.arange(row_count).astype(jnp.float32)[:, None] * frequency[None, :]
    inside = column < ROT
    cosine = jnp.where(inside, jnp.cos(angles), 1.0)
    sine_part = jnp.sin(angles)
    ahead_sin = jnp.where(column < half_rot, -sine_part, 0.0)
    behind_sin = jnp.where(inside & (column >= half_rot), sine_part, 0.0)
    return (cosine, ahead_sin, behind_sin)


def rotate(field, tables):
    cosine, ahead_sin, behind_sin = tables
    half_rot = ROT // 2
    return (
        field * cosine
        + jnp.roll(field, -half_rot, axis=-1) * ahead_sin
        + jnp.roll(field, half_rot, axis=-1) * behind_sin
    )


def pick_rows(gathered, shard_rows, wanted):
    shard_count = shard_rows.shape[0]
    inside = (wanted >= 0) & (wanted < shard_count)
    picked = jnp.take(shard_rows, jnp.clip(wanted, 0, shard_count - 1), axis=0)
    return jnp.where(inside[:, None, None], picked, gathered)


def normalize(rows_in):
    row_mean = jnp.mean(rows_in, -1, keepdims=True)
    centred = rows_in - row_mean
    variance = jnp.mean(centred * centred, -1, keepdims=True)
    inv_scale = lax.rsqrt(variance + eps)
    return (centred * inv_scale, inv_scale)


def block_scores(queries, key_heads, first_row, block_rows, length):
    head_count = key_heads.shape[1]
    query_block = queries[first_row : first_row + block_rows].reshape(
        block_rows, head_count, HEAD_DIM
    )
    scores = jnp.einsum(
        "qhd,khd->hqk", query_block, key_heads, preferred_element_type=jnp.float32
    ) * (1.0 / math.sqrt(HEAD_DIM))
    row_ids = first_row + jnp.arange(block_rows, dtype=jnp.int32)
    col_ids = jnp.arange(key_heads.shape[0], dtype=jnp.int32)
    allowed = (col_ids[None, :] <= row_ids[:, None]) & (col_ids[None, :] < length)
    return (jnp.where(allowed[None], scores, masked_score), query_block)


def attend_forward(inputs):
    queries, key_rows, values, length = inputs
    seq_len = queries.shape[0]
    head_count = queries.shape[1] // HEAD_DIM
    key_heads = key_rows.reshape(seq_len, head_count, HEAD_DIM)
    value_heads = values.reshape(seq_len, head_count, HEAD_DIM)
    block_rows = min(512, seq_len)
    mixed_parts = []
    total_parts = []
    for first_row in range(0, seq_len, block_rows):
        scores, query_block = block_scores(queries, key_heads, first_row, block_rows, length)
        row_max = jnp.max(scores, -1, keepdims=True)
        exped = jnp.exp(scores - row_max)
        row_total = jnp.sum(exped, -1, keepdims=True)
        attn_probs = (exped / row_total).astype(jnp.bfloat16)
        attention_mixture = jnp.einsum(
            "hqk,khd->qhd", attn_probs, value_heads, preferred_element_type=jnp.float32
        )
        mixed_parts.append(attention_mixture.reshape(block_rows, head_count * HEAD_DIM))
        total_parts.append(row_max[..., 0] + jnp.log(row_total[..., 0]))
    return (jnp.concatenate(mixed_parts, 0).astype(jnp.bfloat16), jnp.concatenate(total_parts, 1))


def attend_backward(inputs):
    queries, key_rows, values, log_total, grad_mixed, length = inputs
    seq_len = queries.shape[0]
    head_count = queries.shape[1] // HEAD_DIM
    key_heads = key_rows.reshape(seq_len, head_count, HEAD_DIM)
    value_heads = values.reshape(seq_len, head_count, HEAD_DIM)
    block_rows = min(512, seq_len)
    score_scale = 1.0 / math.sqrt(HEAD_DIM)
    grad_query_parts = []
    grad_keys = jnp.zeros((seq_len, head_count, HEAD_DIM), jnp.float32)
    grad_values = jnp.zeros((seq_len, head_count, HEAD_DIM), jnp.float32)
    for first_row in range(0, seq_len, block_rows):
        scores, query_block = block_scores(queries, key_heads, first_row, block_rows, length)
        attn_probs = jnp.exp(scores - log_total[:, first_row : first_row + block_rows, None])
        grad_block = grad_mixed[first_row : first_row + block_rows].reshape(
            block_rows, head_count, HEAD_DIM
        )
        grad_probs = jnp.einsum(
            "qhd,khd->hqk", grad_block, value_heads, preferred_element_type=jnp.float32
        )
        grad_scores = (
            attn_probs * (grad_probs - jnp.sum(attn_probs * grad_probs, -1, keepdims=True))
        ).astype(jnp.bfloat16)
        grad_query = (
            jnp.einsum("hqk,khd->qhd", grad_scores, key_heads, preferred_element_type=jnp.float32)
            * score_scale
        )
        grad_query_parts.append(grad_query.reshape(block_rows, head_count * HEAD_DIM))
        grad_keys = (
            grad_keys
            + jnp.einsum(
                "hqk,qhd->khd", grad_scores, query_block, preferred_element_type=jnp.float32
            )
            * score_scale
        )
        grad_values = grad_values + jnp.einsum(
            "hqk,qhd->khd",
            attn_probs.astype(jnp.bfloat16),
            grad_block,
            preferred_element_type=jnp.float32,
        )
    return (
        jnp.concatenate(grad_query_parts, 0),
        grad_keys.reshape(seq_len, head_count * HEAD_DIM),
        grad_values.reshape(seq_len, head_count * HEAD_DIM),
    )


def activations(
    layernorm_rows,
    query_key_value_whole,
    first_linear_whole,
    bias_qkv,
    first_linear_bias,
    tables,
    slot_len,
):
    qkv_raw = (
        jnp.einsum(
            "mnv,voe->mnoe",
            layernorm_rows,
            query_key_value_whole,
            preferred_element_type=jnp.float32,
        )
        + bias_qkv
    )
    queries = rotate(qkv_raw[:, :, 0], tables).astype(jnp.bfloat16)
    key_rows = rotate(qkv_raw[:, :, 1], tables).astype(jnp.bfloat16)
    values = qkv_raw[:, :, 2].astype(jnp.bfloat16)
    attention_mixture, log_total = lax.map(attend_forward, (queries, key_rows, values, slot_len))
    pre_act = (
        jnp.einsum(
            "bjp,pv->bjv", layernorm_rows, first_linear_whole, preferred_element_type=jnp.float32
        )
        + first_linear_bias
    )
    hidden = jax.nn.gelu(pre_act, approximate=True).astype(jnp.bfloat16)
    return (queries, key_rows, values, attention_mixture, log_total, pre_act, hidden)


def shards(
    hidden_in,
    cotangent,
    lengths,
    slot_of_seq,
    seq_of_slot,
    qkv_weight,
    out_weight,
    fc1_weight,
    fc2_weight,
    ln_gain,
    ln_bias,
    qkv_bias,
    out_bias,
    fc1_bias,
    fc2_bias,
):
    per_index = hidden_in.shape[0]
    rows_here = hidden_in.shape[1]
    width = hidden_in.shape[2]
    tensor_count = lax.axis_size("tensor")
    tensor_index = lax.axis_index("tensor")
    data_index = lax.axis_index("dp")
    seq_len = rows_here * tensor_count
    heads_local = qkv_weight.shape[2]
    hidden_local = fc1_weight.shape[1]
    my_slots = data_index * per_index + jnp.arange(per_index, dtype=jnp.int32)
    sources = jnp.take(seq_of_slot, my_slots)
    slot_len = jnp.take(lengths, sources)
    targets = jnp.take(slot_of_seq, my_slots)
    routed = pick_rows(
        jnp.zeros_like(hidden_in), lax.all_gather(hidden_in, "dp", axis=0, tiled=True), sources
    )
    gain_full, shift_full, qkv_bias_full, out_bias_full, fc1_bias_full, fc2_bias_full = (
        lax.all_gather(ln_gain, ("dp", "tensor"), axis=0, tiled=True),
        lax.all_gather(ln_bias, ("dp", "tensor"), axis=0, tiled=True),
        lax.all_gather(qkv_bias, ("dp", "tensor"), axis=0, tiled=True),
        lax.all_gather(out_bias, ("dp", "tensor"), axis=0, tiled=True),
        lax.all_gather(fc1_bias, ("dp", "tensor"), axis=0, tiled=True),
        lax.all_gather(fc2_bias, ("dp", "tensor"), axis=0, tiled=True),
    )
    gain_full = gain_full.astype(jnp.float32)
    bias_qkv = lax.dynamic_slice_in_dim(
        qkv_bias_full.astype(jnp.float32).reshape(3, width),
        tensor_index * heads_local,
        heads_local,
        1,
    )
    first_linear_bias = lax.dynamic_slice_in_dim(
        fc1_bias_full.astype(jnp.float32), tensor_index * hidden_local, hidden_local, 0
    )
    slot_rows = routed.astype(jnp.float32)
    normed, inv_scale = normalize(slot_rows)
    ln_local = (normed * gain_full + shift_full.astype(jnp.float32)).astype(jnp.bfloat16)
    ln_full = lax.all_gather(ln_local, "tensor", axis=1, tiled=True)
    query_key_value_whole, output_whole, first_linear_whole, fc2_full = (
        lax.all_gather(qkv_weight, "dp", axis=0, tiled=True),
        lax.all_gather(out_weight, "dp", axis=0, tiled=True),
        lax.all_gather(fc1_weight, "dp", axis=0, tiled=True),
        lax.all_gather(fc2_weight, "dp", axis=0, tiled=True),
    )
    tables = rotary_tables(seq_len, heads_local)
    queries, key_rows, values, attention_mixture, log_total, pre_act, hidden = activations(
        ln_full,
        query_key_value_whole,
        first_linear_whole,
        bias_qkv,
        first_linear_bias,
        tables,
        slot_len,
    )
    partial_value = jnp.einsum(
        "xhj,zj->xhz", attention_mixture, output_whole, preferred_element_type=jnp.float32
    ) + jnp.einsum("slf,ef->sle", hidden, fc2_full, preferred_element_type=jnp.float32)
    summed = lax.psum_scatter(partial_value, "tensor", scatter_dimension=1, tiled=True)
    positions = tensor_index * rows_here + jnp.arange(rows_here, dtype=jnp.int32)
    valid = (positions[None, :] < slot_len[:, None])[:, :, None]
    branch = summed + out_bias_full.astype(jnp.float32) + fc2_bias_full.astype(jnp.float32)
    block_out = (slot_rows + jnp.where(valid, branch, 0.0)).astype(jnp.bfloat16)
    grad_rows = jnp.where(valid, cotangent.astype(jnp.float32), 0.0)
    grad_bias = jnp.sum(grad_rows, axis=(0, 1))
    grad_low = grad_rows.astype(jnp.bfloat16)
    whole_gradient = lax.all_gather(grad_low, "tensor", axis=1, tiled=True)
    grad_mixed = jnp.einsum(
        "wix,xa->wia", whole_gradient, output_whole, preferred_element_type=jnp.float32
    ).astype(jnp.bfloat16)
    output_weight_gradient = jnp.einsum(
        "rav,rac->vc", whole_gradient, attention_mixture, preferred_element_type=jnp.float32
    )
    grad_hidden = jnp.einsum(
        "sle,ef->slf", whole_gradient, fc2_full, preferred_element_type=jnp.float32
    )
    grad_fc2_w = jnp.einsum(
        "sle,slf->ef", whole_gradient, hidden, preferred_element_type=jnp.float32
    )
    _, gelu_pull = jax.vjp(lambda inputs: jax.nn.gelu(inputs, approximate=True), pre_act)
    preactivation_gradient = gelu_pull(grad_hidden)[0].astype(jnp.bfloat16)
    grad_fc1_b = jnp.sum(preactivation_gradient, axis=(0, 1), dtype=jnp.float32)
    first_linear_weight_gradient = jnp.einsum(
        "hwj,hwy->jy", ln_full, preactivation_gradient, preferred_element_type=jnp.float32
    )
    layernorm_gradient = jnp.einsum(
        "mig,qg->miq",
        preactivation_gradient,
        first_linear_whole,
        preferred_element_type=jnp.float32,
    )
    grad_query, grad_keys, grad_values = lax.map(
        attend_backward, (queries, key_rows, values, log_total, grad_mixed, slot_len)
    )
    _, rotate_pull = jax.vjp(lambda field: rotate(field, tables), grad_query)
    query_key_value_gradient = jnp.stack(
        [rotate_pull(grad_query)[0], rotate_pull(grad_keys)[0], grad_values], axis=2
    ).astype(jnp.bfloat16)
    grad_qkv_b = jnp.sum(query_key_value_gradient, axis=(0, 1), dtype=jnp.float32)
    query_key_value_weight_gradient = jnp.einsum(
        "jqm,jqnx->mnx", ln_full, query_key_value_gradient, preferred_element_type=jnp.float32
    )
    layernorm_gradient = layernorm_gradient + jnp.einsum(
        "zrhv,nhv->zrn",
        query_key_value_gradient,
        query_key_value_whole,
        preferred_element_type=jnp.float32,
    )
    grad_ln_rows = lax.psum_scatter(layernorm_gradient, "tensor", scatter_dimension=1, tiled=True)
    grad_gain = jnp.sum(grad_ln_rows * normed, axis=(0, 1))
    grad_shift = jnp.sum(grad_ln_rows, axis=(0, 1))
    grad_norm = grad_ln_rows * gain_full
    grad_from_norm = inv_scale * (
        grad_norm
        - jnp.mean(grad_norm, -1, keepdims=True)
        - normed * jnp.mean(grad_norm * normed, -1, keepdims=True)
    )
    grad_slot = (cotangent.astype(jnp.float32) + grad_from_norm).astype(jnp.bfloat16)
    grad_input = pick_rows(
        jnp.zeros_like(grad_slot), lax.all_gather(grad_slot, "dp", axis=0, tiled=True), targets
    )
    grad_qkv_weight, grad_out_weight, grad_fc1_weight, grad_fc2_weight = (
        lax.psum_scatter(query_key_value_weight_gradient, "dp", scatter_dimension=0, tiled=True),
        lax.psum_scatter(output_weight_gradient, "dp", scatter_dimension=0, tiled=True),
        lax.psum_scatter(first_linear_weight_gradient, "dp", scatter_dimension=0, tiled=True),
        lax.psum_scatter(grad_fc2_w, "dp", scatter_dimension=0, tiled=True),
    )
    full_qkv_b = lax.dynamic_update_slice_in_dim(
        jnp.zeros((3, width), jnp.float32), grad_qkv_b, tensor_index * heads_local, 1
    ).reshape(3 * width)
    full_fc1_b = lax.dynamic_update_slice_in_dim(
        jnp.zeros((hidden_local * tensor_count,), jnp.float32),
        grad_fc1_b,
        tensor_index * hidden_local,
        0,
    )
    small_sums = (
        lax.psum_scatter(grad_gain, ("dp", "tensor"), scatter_dimension=0, tiled=True),
        lax.psum_scatter(grad_shift, ("dp", "tensor"), scatter_dimension=0, tiled=True),
        lax.psum_scatter(full_qkv_b, ("dp", "tensor"), scatter_dimension=0, tiled=True),
        lax.psum_scatter(grad_bias, ("dp", "tensor"), scatter_dimension=0, tiled=True),
        lax.psum_scatter(full_fc1_b, ("dp", "tensor"), scatter_dimension=0, tiled=True),
        lax.psum_scatter(grad_bias, ("dp", "tensor"), scatter_dimension=0, tiled=True),
    )
    return (
        block_out,
        grad_input,
        grad_qkv_weight,
        grad_out_weight,
        grad_fc1_weight,
        grad_fc2_weight,
        small_sums[0],
        small_sums[1],
        small_sums[2],
        small_sums[3],
        small_sums[4],
        small_sums[5],
    )


def solution(mesh):
    in_specs = (
        P("dp", "tensor", None),
        P("dp", "tensor", None),
        P(),
        P(),
        P(),
        P("dp", None, "tensor"),
        P("dp", "tensor"),
        P("dp", "tensor"),
        P("dp", "tensor"),
        P(("dp", "tensor")),
        P(("dp", "tensor")),
        P(("dp", "tensor")),
        P(("dp", "tensor")),
        P(("dp", "tensor")),
        P(("dp", "tensor")),
    )
    out_specs = (
        P("dp", "tensor", None),
        P("dp", "tensor", None),
        P("dp", None, "tensor"),
        P("dp", "tensor"),
        P("dp", "tensor"),
        P("dp", "tensor"),
        P(("dp", "tensor")),
        P(("dp", "tensor")),
        P(("dp", "tensor")),
        P(("dp", "tensor")),
        P(("dp", "tensor")),
        P(("dp", "tensor")),
    )
    return jax.shard_map(shards, mesh=mesh, in_specs=in_specs, out_specs=out_specs, check_vma=False)
```

profile of v0, /device:TPU:0, one launch (start us, length us, event | category | flops | bytes accessed | tf_op | source)
XLA Modules:
  0.0 1402.8 jit_solution(5798299145258276597)
XLA Ops:
  18.2 43.2 %all-reduce.19 = (bf16[2048]{0:T(1024)(128)(2,1)S(1)}, bf16[2048]{0:T(1024)(128)(2,1)S(1)}, bf16[6144]{0:T(1024)(128)(2,1)S(1)}, bf16[2048]{0:T(1024)(128)(2,1)}, bf16[2048]{0:T(1024)(128)(2,1)}) all-reduce(bf16[2048]{0:T(1024)(128)(2,1)S(1)} %dynamic-update-slice.5, ...), channel_id=1, replica_groups=mesh['dp'=8,'tensor'=4] {'dp','tensor'}, use_global_device_ids=true, to_apply=%add.9 | all-reduce | flops 14336 | bytes 57344
  61.4 7.2 all-gather.10.cloned.1.call-done
  77.9 68.1 %all-gather = bf16[32,1,256]{2,1,0:T(2,128)(2,1)S(1)} all-gather(bf16[1,1,256]{2,1,0:T(2,128)(2,1)S(1)} %reshape.1348), channel_id=1, replica_groups=mesh['dp'=8,'tensor'=4] {'dp','tensor'}, dimensions={0}, use_global_device_ids=true | all-gather | bytes 16896 | tf_op jit(solution)/shard_map/all_gather | solution.py:207
  148.2 33.4 %all-gather.22.cloned.1.call-done = bf16[1,1024,2048]{2,1,0:T(8,128)(2,1)} async-done(((bf16[1,256,2048]{2,1,0:T(8,128)(2,1)}), bf16[1,1024,2048]{2,1,0:T(8,128)(2,1)}) %all-gather.22.cloned.1.call-update) | async-done | bytes 4194320 | tf_op jit(solution)/shard_map/all_gather | solution.py:251
  181.5 5.2 fusion.94
  187.8 41.3 %all-gather.14.cloned.1.call-done = bf16[2048,3,512]{0,2,1:T(8,128)(2,1)} async-done(((bf16[256,3,512]{0,2,1:T(8,128)(2,1)}), bf16[2048,3,512]{0,2,1:T(8,128)(2,1)}) %all-gather.14.cloned.1.call-update) | async-done | bytes 6291472 | tf_op jit(solution)/shard_map/all_gather | solution.py:225
  229.1 82.8 %all-gather.12.cloned.1.call-done = bf16[1,1024,2048]{2,1,0:T(8,128)(2,1)} async-done(((bf16[1,256,2048]{2,1,0:T(8,128)(2,1)}), bf16[1,1024,2048]{2,1,0:T(8,128)(2,1)}) %all-gather.12.cloned.1.call-update) | async-done | bytes 4194320 | tf_op jit(solution)/shard_map/all_gather | solution.py:223
  311.9 10.2 add_bitcast_fusion.1
  324.7 9.3 fusion.70
  334.9 8.9 fusion.67
  343.8 3.3 fusion.135
  347.1 3.7 fusion.1
  350.9 7.7 fusion.136
  358.6 7.8 fusion
  367.1 13.1 multiply_reduce_fusion.1
  380.2 11.9 multiply_convert_fusion.1
  392.1 3.2 copy-done.1
  398.2 7.0 convolution_multiply_fusion.1
  405.2 9.5 multiply_reduce_fusion
  414.7 10.8 multiply_convert_fusion
  425.6 6.2 convolution_multiply_fusion
  431.8 5.0 add_multiply_fusion
  436.9 8.0 fusion.40
  446.0 9.4 fusion.81
  455.4 3.4 fusion.11
  458.9 7.6 add_convert_fusion
  466.6 14.7 %fusion.32 = f32[1024,2048]{1,0:T(8,128)} fusion(bf16[2048,2048]{1,0:T(8,128)(2,1)} %all-gather.18.cloned.1.call-done, bf16[1,1024,2048]{2,1,0:T(8,128)(2,1)} %all-gather.12.cloned.1.call-done), kind=kOutput, calls=%fused_computation.50 | convolution fusion | flops 8589934592 | bytes 20971520 | tf_op jit(solution)/shard_map/bjp,pv->bjv/dot_general | solution.py:160
  481.2 19.9 %convert_reduce_fusion = (f32[2048]{0:T(1024)S(1)}, bf16[1024,2048]{1,0:T(8,128)(2,1)}) fusion(f32[1024,2048]{1,0:T(8,128)} %fusion.32, f32[2048]{0:T(1024)S(1)} %copy-done.31, bf16[2048,2048]{1,0:T(8,128)(2,1)} %all-gather.20.cloned.1.call-done, bf16[1,1024,2048]{2,1,0:T(8,128)(2,1)} %all-gather.22.cloned.1.call-done), kind=kOutput, calls=%fused_computation.29 | convolution fusion | flops 8638167040 | bytes 25182208 | tf_op jit(solution)/shard_map/sle,ef->slf/dot_general | solution.py:258
  501.2 11.0 fusion.137
  512.2 10.8 fusion.15
  523.1 17.8 %fusion.127 = f32[1024,2048]{1,0:T(8,128)} fusion(bf16[2048,2048]{1,0:T(8,128)(2,1)} %all-gather.20.cloned.1.call-done, f32[1024,2048]{1,0:T(8,128)} %fusion.32, f32[2048]{0:T(1024)S(1)} %copy-done.31), kind=kOutput, calls=%fused_computation.183 | convolution fusion | flops 8610906112 | bytes 25174016 | tf_op jit(solution)/shard_map/slf,ef->sle/dot_general | solution.py:242
  540.9 7.7 fusion.97
  548.8 4.2 fusion.98
  553.8 9.1 add_bitcast_fusion
  566.4 101.0 %reduce-scatter.9.cloned.1.call-done = f32[1,256,2048]{2,1,0:T(8,128)} async-done(((f32[1,1024,2048]{2,1,0:T(8,128)}), f32[1,256,2048]{2,1,0:T(8,128)}) %reduce-scatter.9.cloned.1.call-update) | async-done | bytes 2097168 | tf_op jit(solution)/shard_map/reduce_scatter | solution.py:293
  667.4 3.5 fusion.60
  670.9 144.1 %reduce-scatter.7.cloned.1.call-done = f32[1,256,2048]{2,1,0:T(8,128)} async-done(((f32[1,1024,2048]{2,1,0:T(8,128)}), f32[1,256,2048]{2,1,0:T(8,128)}) %reduce-scatter.7.cloned.1.call-update) | async-done | bytes 2097168 | tf_op jit(solution)/shard_map/reduce_scatter | solution.py:243
  815.0 5.6 fusion.62
  821.3 6.8 fusion.22
  828.3 12.0 fusion.28
  840.3 16.4 %fusion.20 = f32[2048,2048]{1,0:T(8,128)} fusion(bf16[1,1024,2048]{2,1,0:T(8,128)(2,1)} %all-gather.22.cloned.1.call-done, f32[1024,2048]{1,0:T(8,128)} %fusion.32, f32[2048]{0:T(1024)S(1)} %copy-done.31), kind=kOutput, calls=%fused_computation.38 | convolution fusion | flops 8610906112 | bytes 29368320 | tf_op jit(solution)/shard_map/sle,slf->ef/dot_general | solution.py:261
  856.7 15.2 %fusion.34 = f32[2048,2048]{1,0:T(8,128)} fusion(bf16[1024,2048]{1,0:T(8,128)(2,1)} %get-tuple-element.159, bf16[1,1024,2048]{2,1,0:T(8,128)(2,1)} %all-gather.12.cloned.1.call-done), kind=kOutput, calls=%fused_computation.52 | convolution fusion | flops 8589934592 | bytes 25165824 | tf_op jit(solution)/shard_map/hwj,hwy->jy/dot_general | solution.py:267
  873.8 70.6 %all-reduce.22.cloned.1.call-done = (f32[2048]{0:T(1024)}, f32[2048]{0:T(1024)}, f32[6144]{0:T(1024)}, f32[2048]{0:T(1024)}, f32[8192]{0:T(1024)}) async-done(((f32[2048]{0:T(1024)}, f32[2048]{0:T(1024)}, f32[6144]{0:T(1024)}, f32[2048]{0:T(1024)}, f32[8192]{0:T(1024)}), (f32[2048]{0:T(1024)}, f32[2048]{0:T(1024)}, f32[6144]{0:T(1024)}, f32[2048]{0:T(1024)}, f32[8192]{0:T(1024)})) %all-reduce.22.cloned.1.call-update) | async-done | bytes 81936
  950.3 52.3 %all-gather.24.cloned.1.call-done = bf16[8,256,2048]{2,1,0:T(8,128)(2,1)} async-done(((bf16[1,256,2048]{2,1,0:T(8,128)(2,1)}), bf16[8,256,2048]{2,1,0:T(8,128)(2,1)}) %all-gather.24.cloned.1.call-update) | async-done | bytes 8388624 | tf_op jit(solution)/shard_map/all_gather | solution.py:304
  1005.0 52.9 %reduce-scatter.13.cloned.1.call-done = f32[256,512]{1,0:T(8,128)} async-done(((f32[2048,512]{1,0:T(8,128)}), f32[256,512]{1,0:T(8,128)}) %reduce-scatter.13.cloned.1.call-update) | async-done | bytes 524304 | tf_op jit(solution)/shard_map/reduce_scatter | solution.py:308
  1057.8 96.9 %reduce-scatter.11.cloned.1.call-done = f32[256,3,512]{2,0,1:T(8,128)} async-done(((f32[2048,3,512]{2,0,1:T(8,128)}), f32[256,3,512]{2,0,1:T(8,128)}) %reduce-scatter.11.cloned.1.call-update) | async-done | bytes 1572880 | tf_op jit(solution)/shard_map/reduce_scatter | solution.py:307
  1154.7 120.4 %reduce-scatter.17.cloned.1.call-done = f32[256,2048]{1,0:T(8,128)} async-done(((f32[2048,2048]{1,0:T(8,128)}), f32[256,2048]{1,0:T(8,128)}) %reduce-scatter.17.cloned.1.call-update) | async-done | bytes 2097168 | tf_op jit(solution)/shard_map/reduce_scatter | solution.py:310
  1275.1 120.4 %reduce-scatter.15.cloned.1.call-done = f32[256,2048]{1,0:T(8,128)} async-done(((f32[2048,2048]{1,0:T(8,128)}), f32[256,2048]{1,0:T(8,128)}) %reduce-scatter.15.cloned.1.call-update) | async-done | bytes 2097168 | tf_op jit(solution)/shard_map/reduce_scatter | solution.py:309
  (229 shorter events, 45.2 us)
Async XLA Ops:
  7.2 8.5 copy-start.14
  7.2 9.8 copy-start.47
  7.2 10.0 copy-start.48
  7.2 10.3 copy-start.49
  7.2 10.5 copy-start.50
  7.2 10.7 copy-start.51
  7.2 61.3 %all-gather.10.cloned.1.call-start = ((), (), s32[]{:S(2)}) async-start(), calls=%async_computation.6 | async-start | bytes 9437184 | tf_op jit(solution)/shard_map/all_gather | solution.py:200
  8.0 140.2 %all-gather.16.cloned.1.call-start = ((), (), s32[]{:S(2)}) async-start(), calls=%async_computation.9 | async-start | bytes 2359296 | tf_op jit(solution)/shard_map/all_gather | solution.py:226
  8.7 172.8 %all-gather.22.cloned.1.call-start = ((), (), s32[]{:S(2)}) async-start(), calls=%async_computation.13 | async-start | bytes 5242880 | tf_op jit(solution)/shard_map/all_gather | solution.py:251
  15.6 213.4 %all-gather.14.cloned.1.call-start = ((), (), s32[]{:S(2)}) async-start(), calls=%async_computation.8 | async-start | bytes 7077888 | tf_op jit(solution)/shard_map/all_gather | solution.py:225
  16.8 61.0 %copy-start.52 = (bf16[256]{0:T(256)(128)(2,1)S(1)}, bf16[256]{0:T(256)(128)(2,1)}, u32[]{:S(2)}) copy-start(bf16[256]{0:T(256)(128)(2,1)} %param.30) | copy-start | bytes 1540
  16.9 295.0 %all-gather.12.cloned.1.call-start = ((), (), s32[]{:S(2)}) async-start(), calls=%async_computation.7 | async-start | bytes 5242880 | tf_op jit(solution)/shard_map/all_gather | solution.py:223
  61.4 86.8 %copy-start.21 = (f32[2048]{0:T(1024)}, f32[2048]{0:T(1024)S(1)}, u32[]{:S(2)}) copy-start(f32[2048]{0:T(1024)S(1)} %convert_element_type.189) | copy-start | bytes 24580
  75.2 391.3 %all-gather.18.cloned.1.call-start = ((), (), s32[]{:S(2)}) async-start(), calls=%async_computation.10 | async-start | bytes 9437184 | tf_op jit(solution)/shard_map/all_gather | solution.py:227
  75.8 405.4 %all-gather.20.cloned.1.call-start = ((), (), s32[]{:S(2)}) async-start(), calls=%async_computation.11 | async-start | bytes 9437184 | tf_op jit(solution)/shard_map/all_gather | solution.py:228
  76.6 590.8 %reduce-scatter.9.cloned.1.call-start = ((), (), s32[]{:S(2)}) async-start(), calls=%async_computation.14 | async-start | bytes 10485760 | tf_op jit(solution)/shard_map/reduce_scatter | solution.py:293
  76.6 248.1 %copy-start.40 = (pred[512]{0:T(512)(128)(4,1)}, pred[512]{0:T(512)(128)(4,1)S(1)}, u32[]{:S(2)}) copy-start(pred[512]{0:T(512)(128)(4,1)S(1)} %fusion.121) | copy-start | bytes 1540
  77.2 247.5 %copy-start.38 = (pred[512]{0:T(512)(128)(4,1)}, pred[512]{0:T(512)(128)(4,1)S(1)}, u32[]{:S(2)}) copy-start(pred[512]{0:T(512)(128)(4,1)S(1)} %get-tuple-element.165) | copy-start | bytes 1540
  77.2 247.5 %copy-start.42 = (pred[512]{0:T(512)(128)(4,1)}, pred[512]{0:T(512)(128)(4,1)S(1)}, u32[]{:S(2)}) copy-start(pred[512]{0:T(512)(128)(4,1)S(1)} %get-tuple-element.164) | copy-start | bytes 1540
  334.1 16.7 %copy-start.8 = (bf16[1,512,512]{1,2,0:T(8,128)(2,1)}, bf16[1,512,512]{1,2,0:T(8,128)(2,1)S(1)}, u32[]{:S(2)}) copy-start(bf16[1,512,512]{1,2,0:T(8,128)(2,1)S(1)} %get-tuple-element.142) | copy-start | bytes 1572868
  334.7 9.1 copy-start.13
  347.1 11.5 copy-start.16
  347.1 108.3 %copy-start = (f32[8,512,1024]{2,1,0:T(8,128)}, f32[8,512,1024]{2,1,0:T(8,128)S(1)}, u32[]{:S(2)}) copy-start(f32[8,512,1024]{2,1,0:T(8,128)S(1)} %get-tuple-element.151) | copy-start | bytes 50331652
  358.6 7.8 copy-start.18
  380.2 15.1 %copy-start.9 = (bf16[1,512,512]{1,2,0:T(8,128)(2,1)S(1)}, bf16[1,512,512]{1,2,0:T(8,128)(2,1)}, u32[]{:S(2)}) copy-start(bf16[1,512,512]{1,2,0:T(8,128)(2,1)} %copy-done.8) | copy-start | bytes 1572868
  446.0 9.4 copy-start.11
  466.5 14.7 %copy-start.31 = (f32[2048]{0:T(1024)S(1)}, f32[2048]{0:T(1024)}, u32[]{:S(2)}) copy-start(f32[2048]{0:T(1024)} %dynamic_slice.30) | copy-start | bytes 24580
  481.2 19.9 %copy-start.45 = (bf16[2048,2048]{1,0:T(8,128)(2,1)S(1)}, bf16[2048,2048]{1,0:T(8,128)(2,1)}, u32[]{:S(2)}) copy-start(bf16[2048,2048]{1,0:T(8,128)(2,1)} %all-gather.18.cloned.1.call-done) | copy-start | bytes 25165828
  501.2 11.0 copy-start.3
  501.2 11.0 copy-start.5
  523.0 17.9 %copy-start.17 = (f32[8,512]{1,0:T(8,128)S(1)}, f32[8,512]{1,0:T(8,128)}, u32[]{:S(2)}) copy-start(f32[8,512]{1,0:T(8,128)} %copy-done.16) | copy-start | bytes 49156
  523.0 17.9 %copy-start.24 = (f32[8,512]{1,0:T(8,128)S(1)}, f32[8,512]{1,0:T(8,128)}, u32[]{:S(2)}) copy-start(f32[8,512]{1,0:T(8,128)} %copy-done.23) | copy-start | bytes 49156
  523.1 291.9 %reduce-scatter.7.cloned.1.call-start = ((), (), s32[]{:S(2)}) async-start(), calls=%async_computation.12 | async-start | bytes 10485760 | tf_op jit(solution)/shard_map/reduce_scatter | solution.py:243
  523.1 25.6 %slice-start = ((s8[16777216]{0:T(1024)(128)(4,1)}), s8[4194304]{0:T(1024)(128)(4,1)S(1)}, s32[]{:S(2)}) async-start(s8[16777216]{0:T(1024)(128)(4,1)} %bitcast.125), calls=%async_computation.21 | async-start | bytes 8388608
  523.1 25.6 %slice-start.1 = ((s8[16777216]{0:T(1024)(128)(4,1)}), s8[4194304]{0:T(1024)(128)(4,1)S(1)}, s32[]{:S(2)}) async-start(s8[16777216]{0:T(1024)(128)(4,1)} %bitcast.125), calls=%async_computation.22 | async-start | bytes 8388608
  523.1 25.6 %slice-start.2 = ((s8[16777216]{0:T(1024)(128)(4,1)}), s8[4194304]{0:T(1024)(128)(4,1)S(1)}, s32[]{:S(2)}) async-start(s8[16777216]{0:T(1024)(128)(4,1)} %bitcast.125), calls=%async_computation.23 | async-start | bytes 8388608
  562.9 104.5 %copy-start.22 = (f32[2048]{0:T(1024)S(1)}, f32[2048]{0:T(1024)}, u32[]{:S(2)}) copy-start(f32[2048]{0:T(1024)} %copy-done.21) | copy-start | bytes 24580
  562.9 104.5 %copy-start.28 = (f32[256]{0:T(256)S(1)}, f32[256]{0:T(256)}, u32[]{:S(2)}) copy-start(f32[256]{0:T(256)} %copy-done.27) | copy-start | bytes 3076
  562.9 104.5 %copy-start.30 = (f32[256]{0:T(256)S(1)}, f32[256]{0:T(256)}, u32[]{:S(2)}) copy-start(f32[256]{0:T(256)} %copy-done.29) | copy-start | bytes 3076
  563.0 252.0 %copy-start.37 = (pred[256]{0:T(512)(128)(4,1)S(1)}, pred[256]{0:T(512)(128)(4,1)}, u32[]{:S(2)}) copy-start(pred[256]{0:T(512)(128)(4,1)} %copy-done.36) | copy-start | bytes 772
  563.0 381.4 %all-reduce.22.cloned.1.call-start = ((), (), s32[]{:S(2)}) async-start(), calls=%async_computation.20 | async-start | bytes 163840
  566.4 254.1 %copy-start.20 = (f32[8192]{0:T(1024)}, f32[8192]{0:T(1024)S(1)}, u32[]{:S(2)}) copy-start(f32[8192]{0:T(1024)S(1)} %dynamic_update_slice.20) | copy-start | bytes 98308
  820.6 182.1 %all-gather.24.cloned.1.call-start = ((), (), s32[]{:S(2)}) async-start(), calls=%async_computation.15 | async-start | bytes 9437184 | tf_op jit(solution)/shard_map/all_gather | solution.py:304
  821.3 236.5 %reduce-scatter.13.cloned.1.call-start = ((), (), s32[]{:S(2)}) async-start(), calls=%async_computation.17 | async-start | bytes 4718592 | tf_op jit(solution)/shard_map/reduce_scatter | solution.py:308
  828.2 326.5 %reduce-scatter.11.cloned.1.call-start = ((), (), s32[]{:S(2)}) async-start(), calls=%async_computation.16 | async-start | bytes 14155776 | tf_op jit(solution)/shard_map/reduce_scatter | solution.py:307
  840.3 434.9 %reduce-scatter.17.cloned.1.call-start = ((), (), s32[]{:S(2)}) async-start(), calls=%async_computation.19 | async-start | bytes 18874368 | tf_op jit(solution)/shard_map/reduce_scatter | solution.py:310
  856.7 538.8 %reduce-scatter.15.cloned.1.call-start = ((), (), s32[]{:S(2)}) async-start(), calls=%async_computation.18 | async-start | bytes 18874368 | tf_op jit(solution)/shard_map/reduce_scatter | solution.py:309
  946.4 449.6 %copy-start.56 = (f32[64]{0:T(128)}, f32[64]{0:T(128)S(1)}, u32[]{:S(2)}) copy-start(f32[64]{0:T(128)S(1)} %dynamic-slice.20) | copy-start | bytes 772
  (28 other events, 87.8 us)
Sparse Core Ops, SparseCore 0:
  10.0 58.5 all-gather.9
  70.4 27.8 all-gather.15
  100.5 80.9 all-gather.21
  183.8 45.2 all-gather.13
  231.1 80.7 all-gather.11
  313.6 52.9 all-gather.17
  368.4 54.3 all-gather.19
  523.2 144.2 reduce-scatter.8
  669.8 145.1 reduce-scatter.6
  821.2 123.1 all-reduce.21
  946.9 55.7 all-gather.23
  1006.4 51.3 reduce-scatter.12
  1062.3 92.3 reduce-scatter.10
  1159.1 115.9 reduce-scatter.16
  1279.5 115.9 reduce-scatter.14
where the time goes:
time: 1410 us; the launch traced here: 1400 us
  waiting for transfers between devices  927 us (66%)
  matrix products  227 us (16%)
  blocking collectives  111 us (8%)
  other arithmetic  94 us (7%)
  local copies, waits for them, and re-layouts  26.3 us (2%)
  between operations  17.1 us (1%)
    reduce_scatter x1, waiting for transfers between devices, shards(): lax.psum_scatter(partial_value, 'tensor', scatter_dimension=1, tiled=True)  144 us
    reduce_scatter x1, waiting for transfers between devices, shards(): lax.psum_scatter(grad_fc2_w, 'dp', scatter_dimension=0, tiled=True)  120 us
    reduce_scatter x1, waiting for transfers between devices, shards(): lax.psum_scatter(first_linear_weight_gradient, 'dp', scatter_dimension=0,...  120 us
    reduce_scatter x1, waiting for transfers between devices, shards(): lax.psum_scatter(layernorm_gradient, 'tensor', scatter_dimension=1, tiled...  101 us
    reduce_scatter x1, waiting for transfers between devices, shards(): lax.psum_scatter(query_key_value_weight_gradient, 'dp', scatter_dimension...  96.9 us
    all_gather x1, waiting for transfers between devices, shards(): ln_full = lax.all_gather(ln_local, 'tensor', axis=1, tiled=True)  82.8 us
    unnamed x16, waiting for transfers between devices  74 us
    all_gather x1, blocking collectives, shards(): lax.all_gather(fc1_bias, ('dp', 'tensor'), axis=0, tiled=True)  68.1 us
  transfers between devices with their start and end apart: 15, of which 12 were waited for; matrix products, arithmetic and copies ran while one was open for 21% of the time, Pallas kernels for 0%

commit v1 on v0

--- a/solution.py
+++ b/solution.py
@@ -8,6 +8,12 @@
 ROT = 32
 eps = 1e-05
 masked_score = -1e30
+
+
+def in_order(blocks, dim):
+    shape = list(blocks.shape[1:])
+    shape[dim] *= blocks.shape[0]
+    return jnp.moveaxis(blocks, 0, dim).reshape(shape)
 
 
 def rotary_tables(row_count, col_count):
@@ -248,7 +254,19 @@
     grad_rows = jnp.where(valid, cotangent.astype(jnp.float32), 0.0)
     grad_bias = jnp.sum(grad_rows, axis=(0, 1))
     grad_low = grad_rows.astype(jnp.bfloat16)
-    whole_gradient = lax.all_gather(grad_low, "tensor", axis=1, tiled=True)
+    devices = lax.axis_size("tensor")
+    pairs = [(i, (i + 1) % devices) for i in range(devices)]
+    back = [(b, a) for a, b in pairs]
+    lower, upper = ([], [])
+    for lap in range(devices - 1):
+        if lap % 2 == 0:
+            lower.append(lax.ppermute(lower[-1] if lower else grad_low, "tensor", pairs))
+        else:
+            upper.append(lax.ppermute(upper[-1] if upper else grad_low, "tensor", back))
+    blocks = jnp.stack([*lower[::-1], grad_low, *upper])
+    shift = lax.axis_index("tensor") - len(lower)
+    blocks = blocks[(jnp.arange(devices) - shift) % devices]
+    whole_gradient = in_order(blocks, 1)
     grad_mixed = jnp.einsum(
         "wix,xa->wia", whole_gradient, output_whole, preferred_element_type=jnp.float32
     ).astype(jnp.bfloat16)

time: 1410 us -> 1330 us (0.943)
  waiting for transfers between devices: 927 us -> 793 us
  blocking collectives: 111 us -> 147 us
    all_gather x1, waiting for transfers between devices: 82.8 us -> 3.83 us  [shards(): ln_full = lax.all_gather(ln_local, 'tensor', axis=1, tiled=True)]
    all_gather x1, waiting for transfers between devices: 41.3 us -> 0.01 us  [shards(): lax.all_gather(qkv_weight, 'dp', axis=0, tiled=True)]
    all_gather x1, blocking collectives: 68.1 us -> 104 us  [shards(): lax.all_gather(fc1_bias, ('dp', 'tensor'), axis=0, tiled=True)]
    all_gather x1 -> x0, waiting for transfers between devices: 33.4 us -> none  [shards(): whole_gradient = lax.all_gather(grad_low, 'tensor', axis=1, tiled=True)]
    ppermute x0 -> x3, waiting for transfers between devices: none -> 22.7 us  [the longest x2 22.7 us: shards(): lax.ppermute(lower[-1] if lower else grad_low, 'tensor', pairs)]
    unnamed x16 -> x15, waiting for transfers between devices: 74 us -> 72 us
  transfers between devices with their start and end apart: 15 -> 17, of which waited for: 12 -> 11; matrix products, arithmetic and copies ran while one was open for 21% -> 23% of each run, Pallas kernels for 0% -> 0%
where the time goes in v1:
time: 1330 us; the launch traced here: 1320 us
  waiting for transfers between devices  793 us (60%)
  matrix products  227 us (17%)
  blocking collectives  147 us (11%)
  other arithmetic  97 us (7%)
  local copies, waits for them, and re-layouts  35 us (3%)
  between operations  17.1 us (1%)
    reduce_scatter x1, waiting for transfers between devices, shards(): lax.psum_scatter(partial_value, 'tensor', scatter_dimension=1, tiled=True)  144 us
    reduce_scatter x1, waiting for transfers between devices, shards(): lax.psum_scatter(grad_fc2_w, 'dp', scatter_dimension=0, tiled=True)  121 us
    reduce_scatter x1, waiting for transfers between devices, shards(): lax.psum_scatter(first_linear_weight_gradient, 'dp', scatter_dimension=0,...  120 us
    all_gather x1, blocking collectives, shards(): lax.all_gather(fc1_bias, ('dp', 'tensor'), axis=0, tiled=True)  104 us
    reduce_scatter x1, waiting for transfers between devices, shards(): lax.psum_scatter(layernorm_gradient, 'tensor', scatter_dimension=1, tiled...  99.9 us
    reduce_scatter x1, waiting for transfers between devices, shards(): lax.psum_scatter(query_key_value_weight_gradient, 'dp', scatter_dimension...  96.8 us
    unnamed x15, waiting for transfers between devices  72 us
    reduce_scatter x1, waiting for transfers between devices, shards(): lax.psum_scatter(output_weight_gradient, 'dp', scatter_dimension=0, tiled...  53 us
  transfers between devices with their start and end apart: 17, of which 11 were waited for; matrix products, arithmetic and copies ran while one was open for 23% of the time, Pallas kernels for 0%

profile of v1, /device:TPU:0, one launch (start us, length us, event | category | flops | bytes accessed | tf_op | source)
XLA Modules:
  0.0 1321.3 jit_solution(426264339516935768)
XLA Ops:
  17.3 43.2 %all-reduce.19 = (bf16[2048]{0:T(1024)(128)(2,1)S(1)}, bf16[2048]{0:T(1024)(128)(2,1)S(1)}, bf16[6144]{0:T(1024)(128)(2,1)S(1)}, bf16[2048]{0:T(1024)(128)(2,1)}, bf16[2048]{0:T(1024)(128)(2,1)}) all-reduce(bf16[2048]{0:T(1024)(128)(2,1)S(1)} %dynamic-update-slice.5, ...), channel_id=1, replica_groups=mesh['dp'=8,'tensor'=4] {'dp','tensor'}, use_global_device_ids=true, to_apply=%add.9 | all-reduce | flops 14336 | bytes 57344
  60.6 7.9 all-gather.9.cloned.1.call-done
  82.5 22.7 %collective-permute-done = bf16[1,256,2048]{2,1,0:T(8,128)(2,1)S(1)} collective-permute-done((bf16[1,256,2048]{2,1,0:T(8,128)(2,1)S(1)}, bf16[1,256,2048]{2,1,0:T(8,128)(2,1)S(1)}, u32[]{:S(2)}, u32[]{:S(2)}) %collective-permute-start) | collective-permute-done | bytes 1048608 | tf_op jit(solution)/shard_map/ppermute | solution.py:263
  105.2 104.1 %all-gather = bf16[32,1,256]{2,1,0:T(2,128)(2,1)S(1)} all-gather(bf16[1,1,256]{2,1,0:T(2,128)(2,1)S(1)} %reshape.1412), channel_id=1, replica_groups=mesh['dp'=8,'tensor'=4] {'dp','tensor'}, dimensions={0}, use_global_device_ids=true | all-gather | bytes 16896 | tf_op jit(solution)/shard_map/all_gather | solution.py:213
  211.7 3.5 maximum_bitcast_fusion
  215.2 5.1 gather_fusion
  220.3 5.2 fusion.81
  226.6 3.8 all-gather.11.cloned.1.call-done
  230.4 10.1 add_bitcast_fusion.1
  243.1 9.3 fusion.60
  253.3 9.1 fusion.57
  262.4 3.3 fusion.125
  265.7 3.7 fusion.1
  269.5 7.6 fusion.126
  277.1 7.8 fusion
  285.6 13.1 multiply_reduce_fusion.1
  298.7 12.3 multiply_convert_fusion.1
  317.2 7.0 convolution_multiply_fusion.1
  324.2 9.5 multiply_reduce_fusion
  333.7 10.4 multiply_convert_fusion
  344.1 6.2 convolution_multiply_fusion
  350.3 5.0 add_multiply_fusion
  355.4 8.0 fusion.30
  364.5 9.6 fusion.71
  374.1 3.4 fusion.11
  377.6 7.6 add_convert_fusion
  385.2 14.5 %fusion.24 = f32[1024,2048]{1,0:T(8,128)} fusion(bf16[2048,2048]{1,0:T(8,128)(2,1)} %all-gather.17.cloned.1.call-done, bf16[1,1024,2048]{2,1,0:T(8,128)(2,1)} %all-gather.11.cloned.1.call-done), kind=kOutput, calls=%fused_computation.44 | convolution fusion | flops 8589934592 | bytes 20971520 | tf_op jit(solution)/shard_map/bjp,pv->bjv/dot_general | solution.py:166
  399.8 19.9 %convert_reduce_fusion = (f32[2048]{0:T(1024)S(1)}, bf16[1024,2048]{1,0:T(8,128)(2,1)}) fusion(f32[1024,2048]{1,0:T(8,128)} %fusion.24, f32[2048]{0:T(1024)S(1)} %copy-done.32, bf16[1024,2048]{1,0:T(8,128)(2,1)} %bitcast.153, bf16[2048,2048]{1,0:T(8,128)(2,1)} %all-gather.19.cloned.1.call-done), kind=kOutput, calls=%fused_computation.30 | convolution fusion | flops 8638167040 | bytes 25182208 | tf_op jit(solution)/shard_map/sle,ef->slf/dot_general | solution.py:276
  419.7 10.8 fusion.127
  430.6 11.0 fusion.15
  441.7 18.1 %fusion.116 = f32[1024,2048]{1,0:T(8,128)} fusion(bf16[2048,2048]{1,0:T(8,128)(2,1)} %all-gather.19.cloned.1.call-done, f32[1024,2048]{1,0:T(8,128)} %fusion.24, f32[2048]{0:T(1024)S(1)} %copy-done.32), kind=kOutput, calls=%fused_computation.186 | convolution fusion | flops 8610906112 | bytes 25174016 | tf_op jit(solution)/shard_map/slf,ef->sle/dot_general | solution.py:248
  459.8 7.7 fusion.82
  467.7 4.2 fusion.83
  472.7 9.0 add_bitcast_fusion
  485.9 99.9 %reduce-scatter.9.cloned.1.call-done = f32[1,256,2048]{2,1,0:T(8,128)} async-done(((f32[1,1024,2048]{2,1,0:T(8,128)}), f32[1,256,2048]{2,1,0:T(8,128)}) %reduce-scatter.9.cloned.1.call-update) | async-done | bytes 2097168 | tf_op jit(solution)/shard_map/reduce_scatter | solution.py:311
  585.8 3.5 fusion.50
  589.4 144.1 %reduce-scatter.7.cloned.1.call-done = f32[1,256,2048]{2,1,0:T(8,128)} async-done(((f32[1,1024,2048]{2,1,0:T(8,128)}), f32[1,256,2048]{2,1,0:T(8,128)}) %reduce-scatter.7.cloned.1.call-update) | async-done | bytes 2097168 | tf_op jit(solution)/shard_map/reduce_scatter | solution.py:249
  733.4 5.4 fusion.52
  739.5 6.9 fusion.84
  747.6 11.9 fusion.20
  759.6 16.6 %fusion.115 = f32[2048,2048]{1,0:T(8,128)} fusion(bf16[1024,2048]{1,0:T(8,128)(2,1)} %bitcast.155, f32[1024,2048]{1,0:T(8,128)} %fusion.24, f32[2048]{0:T(1024)S(1)} %copy-done.32), kind=kOutput, calls=%fused_computation.185 | convolution fusion | flops 8610906112 | bytes 29368320 | tf_op jit(solution)/shard_map/sle,slf->ef/dot_general | solution.py:279
  776.3 15.3 %fusion.26 = f32[2048,2048]{1,0:T(8,128)} fusion(bf16[1024,2048]{1,0:T(8,128)(2,1)} %get-tuple-element.123, bf16[1,1024,2048]{2,1,0:T(8,128)(2,1)} %all-gather.11.cloned.1.call-done), kind=kOutput, calls=%fused_computation.46 | convolution fusion | flops 8589934592 | bytes 25165824 | tf_op jit(solution)/shard_map/hwj,hwy->jy/dot_general | solution.py:285
  793.5 69.4 %all-reduce.22.cloned.1.call-done = (f32[2048]{0:T(1024)}, f32[2048]{0:T(1024)}, f32[6144]{0:T(1024)}, f32[2048]{0:T(1024)}, f32[8192]{0:T(1024)}) async-done(((f32[2048]{0:T(1024)}, f32[2048]{0:T(1024)}, f32[6144]{0:T(1024)}, f32[2048]{0:T(1024)}, f32[8192]{0:T(1024)}), (f32[2048]{0:T(1024)}, f32[2048]{0:T(1024)}, f32[6144]{0:T(1024)}, f32[2048]{0:T(1024)}, f32[8192]{0:T(1024)})) %all-reduce.22.cloned.1.call-update) | async-done | bytes 81936
  868.8 52.2 %all-gather.21.cloned.1.call-done = bf16[8,256,2048]{2,1,0:T(8,128)(2,1)} async-done(((bf16[1,256,2048]{2,1,0:T(8,128)(2,1)}), bf16[8,256,2048]{2,1,0:T(8,128)(2,1)}) %all-gather.21.cloned.1.call-update) | async-done | bytes 8388624 | tf_op jit(solution)/shard_map/all_gather | solution.py:322
  923.3 53.0 %reduce-scatter.13.cloned.1.call-done = f32[256,512]{1,0:T(8,128)} async-done(((f32[2048,512]{1,0:T(8,128)}), f32[256,512]{1,0:T(8,128)}) %reduce-scatter.13.cloned.1.call-update) | async-done | bytes 524304 | tf_op jit(solution)/shard_map/reduce_scatter | solution.py:326
  976.3 96.8 %reduce-scatter.11.cloned.1.call-done = f32[256,3,512]{2,0,1:T(8,128)} async-done(((f32[2048,3,512]{2,0,1:T(8,128)}), f32[256,3,512]{2,0,1:T(8,128)}) %reduce-scatter.11.cloned.1.call-update) | async-done | bytes 1572880 | tf_op jit(solution)/shard_map/reduce_scatter | solution.py:325
  1073.1 120.6 %reduce-scatter.17.cloned.1.call-done = f32[256,2048]{1,0:T(8,128)} async-done(((f32[2048,2048]{1,0:T(8,128)}), f32[256,2048]{1,0:T(8,128)}) %reduce-scatter.17.cloned.1.call-update) | async-done | bytes 2097168 | tf_op jit(solution)/shard_map/reduce_scatter | solution.py:328
  1193.6 120.4 %reduce-scatter.15.cloned.1.call-done = f32[256,2048]{1,0:T(8,128)} async-done(((f32[2048,2048]{1,0:T(8,128)}), f32[256,2048]{1,0:T(8,128)}) %reduce-scatter.15.cloned.1.call-update) | async-done | bytes 2097168 | tf_op jit(solution)/shard_map/reduce_scatter | solution.py:327
  (231 shorter events, 54.2 us)
Async XLA Ops:
  7.2 61.2 %all-gather.9.cloned.1.call-start = ((), (), s32[]{:S(2)}) async-start(), calls=%async_computation.6 | async-start | bytes 9437184 | tf_op jit(solution)/shard_map/all_gather | solution.py:206
  7.9 212.4 %all-gather.15.cloned.1.call-start = ((), (), s32[]{:S(2)}) async-start(), calls=%async_computation.9 | async-start | bytes 2359296 | tf_op jit(solution)/shard_map/all_gather | solution.py:232
  8.7 67.1 %copy-start.48 = (s32[8]{0:T(128)S(1)}, s32[8]{0:T(128)}, u32[]{:S(2)}) copy-start(s32[8]{0:T(128)} %param.19) | copy-start | bytes 100
  8.7 68.4 %copy-start.3 = (bf16[1,256,2048]{2,1,0:T(8,128)(2,1)S(1)}, bf16[1,256,2048]{2,1,0:T(8,128)(2,1)}, u32[]{:S(2)}) copy-start(bf16[1,256,2048]{2,1,0:T(8,128)(2,1)} %param.18) | copy-start | bytes 3145732
  8.7 217.9 %all-gather.13.cloned.1.call-start = ((), (), s32[]{:S(2)}) async-start(), calls=%async_computation.8 | async-start | bytes 7077888 | tf_op jit(solution)/shard_map/all_gather | solution.py:231
  11.1 219.3 %all-gather.11.cloned.1.call-start = ((), (), s32[]{:S(2)}) async-start(), calls=%async_computation.7 | async-start | bytes 5242880 | tf_op jit(solution)/shard_map/all_gather | solution.py:229
  60.6 16.5 %copy-start.22 = (f32[2048]{0:T(1024)}, f32[2048]{0:T(1024)S(1)}, u32[]{:S(2)}) copy-start(f32[2048]{0:T(1024)S(1)} %convert_element_type.189) | copy-start | bytes 24580
  70.0 35.2 %copy-start.49 = (bf16[256]{0:T(256)(128)(2,1)S(1)}, bf16[256]{0:T(256)(128)(2,1)}, u32[]{:S(2)}) copy-start(bf16[256]{0:T(256)(128)(2,1)} %param.30) | copy-start | bytes 1540
  75.1 310.1 %all-gather.17.cloned.1.call-start = ((), (), s32[]{:S(2)}) async-start(), calls=%async_computation.10 | async-start | bytes 9437184 | tf_op jit(solution)/shard_map/all_gather | solution.py:233
  75.7 324.1 %all-gather.19.cloned.1.call-start = ((), (), s32[]{:S(2)}) async-start(), calls=%async_computation.11 | async-start | bytes 9437184 | tf_op jit(solution)/shard_map/all_gather | solution.py:234
  77.0 138.1 %copy-start.33 = (pred[256]{0:T(512)(128)(4,1)}, pred[256]{0:T(512)(128)(4,1)S(1)}, u32[]{:S(2)}) copy-start(pred[256]{0:T(512)(128)(4,1)S(1)} %add_compare_fusion) | copy-start | bytes 772
  77.3 27.9 %collective-permute-start = (bf16[1,256,2048]{2,1,0:T(8,128)(2,1)S(1)}, bf16[1,256,2048]{2,1,0:T(8,128)(2,1)S(1)}, u32[]{:S(2)}, u32[]{:S(2)}) collective-permute-start(bf16[1,256,2048]{2,1,0:T(8,128)(2,1)S(1)} %fusion.36), channel_id=1, source_target_pairs={{0,1},{1,2},{2,3},{3,0},{4,5},{5,6},{6,7},{7,4},{8,9},{9,10},{10,1... | collective-permute-start | bytes 3145736 | tf_op jit(solution)/shard_map/ppermute | solution.py:263
  78.8 132.8 %collective-permute-start.2 = (bf16[1,256,2048]{2,1,0:T(8,128)(2,1)S(1)}, bf16[1,256,2048]{2,1,0:T(8,128)(2,1)}, u32[]{:S(2)}, u32[]{:S(2)}) collective-permute-start(bf16[1,256,2048]{2,1,0:T(8,128)(2,1)S(1)} %fusion.36), channel_id=1, source_target_pairs={{1,0},{2,1},{3,2},{0,3},{5,4},{6,5},{7,6},{4,7},{9,8},{10,9},{11,1... | collective-permute-start | bytes 3145736 | tf_op jit(solution)/shard_map/ppermute | solution.py:265
  81.2 504.6 %reduce-scatter.9.cloned.1.call-start = ((), (), s32[]{:S(2)}) async-start(), calls=%async_computation.13 | async-start | bytes 10485760 | tf_op jit(solution)/shard_map/reduce_scatter | solution.py:311
  81.3 161.8 %copy-start.41 = (pred[512]{0:T(512)(128)(4,1)}, pred[512]{0:T(512)(128)(4,1)S(1)}, u32[]{:S(2)}) copy-start(pred[512]{0:T(512)(128)(4,1)S(1)} %fusion.107) | copy-start | bytes 1540
  81.9 161.2 %copy-start.39 = (pred[512]{0:T(512)(128)(4,1)}, pred[512]{0:T(512)(128)(4,1)S(1)}, u32[]{:S(2)}) copy-start(pred[512]{0:T(512)(128)(4,1)S(1)} %get-tuple-element.165) | copy-start | bytes 1540
  81.9 161.3 %copy-start.43 = (pred[512]{0:T(512)(128)(4,1)}, pred[512]{0:T(512)(128)(4,1)S(1)}, u32[]{:S(2)}) copy-start(pred[512]{0:T(512)(128)(4,1)S(1)} %get-tuple-element.164) | copy-start | bytes 1540
  105.2 106.5 %collective-permute-start.1 = (bf16[1,256,2048]{2,1,0:T(8,128)(2,1)S(1)}, bf16[1,256,2048]{2,1,0:T(8,128)(2,1)}, u32[]{:S(2)}, u32[]{:S(2)}) collective-permute-start(bf16[1,256,2048]{2,1,0:T(8,128)(2,1)S(1)} %collective-permute-done), channel_id=1, source_target_pairs={{0,1},{1,2},{2,3},{3,0},{4,5},{5,6},{6,7},{7,4},{8,9},{9,10},{10,1... | collective-permute-start | bytes 3145736 | tf_op jit(solution)/shard_map/ppermute | solution.py:263
  252.5 16.9 %copy-start.10 = (bf16[1,512,512]{1,2,0:T(8,128)(2,1)}, bf16[1,512,512]{1,2,0:T(8,128)(2,1)S(1)}, u32[]{:S(2)}) copy-start(bf16[1,512,512]{1,2,0:T(8,128)(2,1)S(1)} %get-tuple-element.144) | copy-start | bytes 1572868
  253.1 9.3 copy-start.15
  265.7 11.4 copy-start.17
  265.7 108.4 %copy-start = (f32[8,512,1024]{2,1,0:T(8,128)}, f32[8,512,1024]{2,1,0:T(8,128)S(1)}, u32[]{:S(2)}) copy-start(f32[8,512,1024]{2,1,0:T(8,128)S(1)} %get-tuple-element.153) | copy-start | bytes 50331652
  277.1 7.8 copy-start.19
  298.7 15.6 %copy-start.11 = (bf16[1,512,512]{1,2,0:T(8,128)(2,1)S(1)}, bf16[1,512,512]{1,2,0:T(8,128)(2,1)}, u32[]{:S(2)}) copy-start(bf16[1,512,512]{1,2,0:T(8,128)(2,1)} %copy-done.10) | copy-start | bytes 1572868
  364.5 9.6 copy-start.13
  385.2 14.6 %copy-start.32 = (f32[2048]{0:T(1024)S(1)}, f32[2048]{0:T(1024)}, u32[]{:S(2)}) copy-start(f32[2048]{0:T(1024)} %dynamic_slice.30) | copy-start | bytes 24580
  399.8 19.9 %copy-start.46 = (bf16[2048,2048]{1,0:T(8,128)(2,1)S(1)}, bf16[2048,2048]{1,0:T(8,128)(2,1)}, u32[]{:S(2)}) copy-start(bf16[2048,2048]{1,0:T(8,128)(2,1)} %all-gather.17.cloned.1.call-done) | copy-start | bytes 25165828
  419.7 10.8 copy-start.5
  419.7 10.8 copy-start.7
  441.6 18.2 %copy-start.18 = (f32[8,512]{1,0:T(8,128)S(1)}, f32[8,512]{1,0:T(8,128)}, u32[]{:S(2)}) copy-start(f32[8,512]{1,0:T(8,128)} %copy-done.17) | copy-start | bytes 49156
  441.6 18.2 %copy-start.25 = (f32[8,512]{1,0:T(8,128)S(1)}, f32[8,512]{1,0:T(8,128)}, u32[]{:S(2)}) copy-start(f32[8,512]{1,0:T(8,128)} %copy-done.24) | copy-start | bytes 49156
  441.6 291.8 %reduce-scatter.7.cloned.1.call-start = ((), (), s32[]{:S(2)}) async-start(), calls=%async_computation.12 | async-start | bytes 10485760 | tf_op jit(solution)/shard_map/reduce_scatter | solution.py:249
  441.7 25.9 %slice-start = ((s8[16777216]{0:T(1024)(128)(4,1)}), s8[4194304]{0:T(1024)(128)(4,1)S(1)}, s32[]{:S(2)}) async-start(s8[16777216]{0:T(1024)(128)(4,1)} %bitcast.122), calls=%async_computation.20 | async-start | bytes 8388608
  441.7 25.9 %slice-start.1 = ((s8[16777216]{0:T(1024)(128)(4,1)}), s8[4194304]{0:T(1024)(128)(4,1)S(1)}, s32[]{:S(2)}) async-start(s8[16777216]{0:T(1024)(128)(4,1)} %bitcast.122), calls=%async_computation.21 | async-start | bytes 8388608
  441.7 25.9 %slice-start.2 = ((s8[16777216]{0:T(1024)(128)(4,1)}), s8[4194304]{0:T(1024)(128)(4,1)S(1)}, s32[]{:S(2)}) async-start(s8[16777216]{0:T(1024)(128)(4,1)} %bitcast.122), calls=%async_computation.22 | async-start | bytes 8388608
  481.8 104.0 %copy-start.23 = (f32[2048]{0:T(1024)S(1)}, f32[2048]{0:T(1024)}, u32[]{:S(2)}) copy-start(f32[2048]{0:T(1024)} %copy-done.22) | copy-start | bytes 24580
  481.8 104.0 %copy-start.29 = (f32[256]{0:T(256)S(1)}, f32[256]{0:T(256)}, u32[]{:S(2)}) copy-start(f32[256]{0:T(256)} %copy-done.28) | copy-start | bytes 3076
  481.8 104.0 %copy-start.31 = (f32[256]{0:T(256)S(1)}, f32[256]{0:T(256)}, u32[]{:S(2)}) copy-start(f32[256]{0:T(256)} %copy-done.30) | copy-start | bytes 3076
  481.8 251.6 %copy-start.4 = (bf16[1,256,2048]{2,1,0:T(8,128)(2,1)S(1)}, bf16[1,256,2048]{2,1,0:T(8,128)(2,1)}, u32[]{:S(2)}) copy-start(bf16[1,256,2048]{2,1,0:T(8,128)(2,1)} %param.18) | copy-start | bytes 3145732
  481.8 251.6 %copy-start.34 = (pred[256]{0:T(512)(128)(4,1)S(1)}, pred[256]{0:T(512)(128)(4,1)}, u32[]{:S(2)}) copy-start(pred[256]{0:T(512)(128)(4,1)} %copy-done.33) | copy-start | bytes 772
  481.9 381.1 %all-reduce.22.cloned.1.call-start = ((), (), s32[]{:S(2)}) async-start(), calls=%async_computation.19 | async-start | bytes 163840
  485.9 252.9 %copy-start.21 = (f32[8192]{0:T(1024)}, f32[8192]{0:T(1024)S(1)}, u32[]{:S(2)}) copy-start(f32[8192]{0:T(1024)S(1)} %dynamic_update_slice.20) | copy-start | bytes 98308
  738.8 182.2 %all-gather.21.cloned.1.call-start = ((), (), s32[]{:S(2)}) async-start(), calls=%async_computation.14 | async-start | bytes 9437184 | tf_op jit(solution)/shard_map/all_gather | solution.py:322
  739.4 236.9 %reduce-scatter.13.cloned.1.call-start = ((), (), s32[]{:S(2)}) async-start(), calls=%async_computation.16 | async-start | bytes 4718592 | tf_op jit(solution)/shard_map/reduce_scatter | solution.py:326
  746.4 326.7 %reduce-scatter.11.cloned.1.call-start = ((), (), s32[]{:S(2)}) async-start(), calls=%async_computation.15 | async-start | bytes 14155776 | tf_op jit(solution)/shard_map/reduce_scatter | solution.py:325
  759.5 434.1 %reduce-scatter.17.cloned.1.call-start = ((), (), s32[]{:S(2)}) async-start(), calls=%async_computation.18 | async-start | bytes 18874368 | tf_op jit(solution)/shard_map/reduce_scatter | solution.py:328
  776.2 537.8 %reduce-scatter.15.cloned.1.call-start = ((), (), s32[]{:S(2)}) async-start(), calls=%async_computation.17 | async-start | bytes 18874368 | tf_op jit(solution)/shard_map/reduce_scatter | solution.py:327
  864.9 449.6 %copy-start.53 = (f32[64]{0:T(128)}, f32[64]{0:T(128)S(1)}, u32[]{:S(2)}) copy-start(f32[64]{0:T(128)S(1)} %dynamic-slice.20) | copy-start | bytes 772
  (27 other events, 86.8 us)
Sparse Core Ops, SparseCore 0:
  9.9 58.4 all-gather.8
  70.3 27.9 all-gather.14
  100.7 46.6 all-gather.12
  149.4 80.9 all-gather.10
  232.2 53.0 all-gather.16
  287.0 54.3 all-gather.18
  441.7 144.0 reduce-scatter.8
  588.2 145.1 reduce-scatter.6
  739.9 123.0 all-reduce.21
  865.2 55.7 all-gather.20
  925.0 51.3 reduce-scatter.12
  980.7 92.3 reduce-scatter.10
  1077.7 115.9 reduce-scatter.16
  1198.1 115.9 reduce-scatter.14
